TPU v7x, 256 devices: a whole 4x4x8 slice. The times are simulated.
256 devices in a mesh: seq: 128 (over y, x_lo, z, core), mp: 2 (over x_hi).
Axes of the slice: x: 4 (x_hi: 2, x_lo: 2; x = x_hi * 2 + x_lo), y: 4, z: 8, core: 2. Of those that a mesh axis runs over, the one named last changes fastest.
Arguments:
- normed: bfloat16 [65536, 2048], P('seq', 'mp'), may hold values from -18 to 18
- router: bfloat16 [2048], replicated, may hold values from -0.125 to 0.125
- light_qkv: bfloat16 [3, 2048, 1024], P(None, None, 'mp'), may hold values from -0.125 to 0.125
- light_out: bfloat16 [1024, 2048], P('mp'), may hold values from -0.1875 to 0.1875
- heavy_qkv: bfloat16 [3, 2048, 1024], P(None, 'seq', 'mp'), may hold values from -0.125 to 0.125
- heavy_out: bfloat16 [1024, 2048], P('mp', 'seq'), may hold values from -0.1875 to 0.1875
- query_slots: int32 [128, 32], P('seq'), may hold values from 0 to 511, as said below
- query_count: int32 [128], P('seq'), may hold values from 1 to 32, 2048 in all
- key_slots: int32 [128, 32], P('seq'), may hold values from 0 to 511, as said below
- key_count: int32 [128], P('seq'), may hold values from 1 to 32, 2048 in all
Outputs:
- mixed: bfloat16 [65536, 2048], P('seq', 'mp')
Inputs may be any that keep to these rules, and one draw needn't show every extreme that they name: `query_slots`: each row holds 32 distinct positions of one shard's 512 tokens; only the first query_count entries of a row are live. `key_slots`: each row holds 32 distinct positions of one shard's 512 tokens; only the first key_count entries of a row are live. `query_count`: the counts sum to 2048 and the largest is exactly 32. `key_count`: the counts sum to 2048 and the largest is exactly 32.
All inputs are finite; a program needn't handle non-finite values.
Results may differ from a plain program's by a relative error of at most 0.012.
Values may be sent and summed in bfloat16 or wider, within the bound.
No kernel may reach another device: no remote copies, remote signals or barrier semaphores. Data moves between devices by JAX's collectives and lax.ppermute only.
A program may use at most 128 MiB of HBM per device.

v0:
```python
import jax
import jax.numpy as jnp
from jax import lax
from jax.sharding import PartitionSpec as P

HEAD_DIM = 64
RADIUS = 64
NEG = -1e30


def padded(cells, sides, width):
    for axis, dim in sides:
        count = lax.axis_size(axis)
        ends = count - 1
        head = lax.slice_in_dim(cells, 0, width, axis=dim)
        tail = lax.slice_in_dim(cells, cells.shape[dim] - width, cells.shape[dim], axis=dim)
        cells = jnp.concatenate(
            [
                lax.ppermute(tail, axis, [(i, (i + 1) % count) for i in range(ends)]),
                cells,
                lax.ppermute(head, axis, [((i + 1) % count, i) for i in range(ends)]),
            ],
            axis=dim,
        )
    return cells


def mix_heads(queries, key_rows, value_rows, allowed):
    length = queries.shape[0]
    head_count = queries.shape[1] // HEAD_DIM
    query_heads = queries.reshape(length, head_count, HEAD_DIM)
    key_heads = key_rows.reshape(key_rows.shape[0], head_count, HEAD_DIM)
    value_heads = value_rows.reshape(value_rows.shape[0], head_count, HEAD_DIM)
    scores = jnp.einsum(
        "qhe,khe->hqk", query_heads, key_heads, preferred_element_type=jnp.float32
    ) * HEAD_DIM ** (-0.5)
    scores = jnp.where(allowed[None], scores, NEG)
    row_peak = jnp.max(scores, axis=2, keepdims=True)
    weights = jnp.where(allowed[None], jnp.exp(scores - row_peak), 0.0)
    row_total = jnp.sum(weights, axis=2)
    blended = jnp.einsum(
        "hqk,khe->qhe",
        weights.astype(jnp.bfloat16),
        value_heads,
        preferred_element_type=jnp.float32,
    )
    blended = blended / jnp.transpose(row_total)[:, :, None]
    return blended.reshape(length, head_count * HEAD_DIM).astype(jnp.bfloat16)


def shards(
    normed,
    router,
    light_qkv,
    light_out,
    heavy_qkv,
    heavy_out,
    query_slots,
    query_count,
    key_slots,
    key_count,
):
    local_rows = normed.shape[0]
    shard_index = lax.axis_index("seq")
    shard_total = lax.axis_size("seq")
    capacity = query_slots.shape[1]
    features = lax.all_gather(normed, "mp", axis=1, tiled=True)
    queries = jnp.dot(features, light_qkv[0], preferred_element_type=jnp.float32).astype(
        jnp.bfloat16
    )
    paired = jnp.einsum(
        "td,cdh->cth", features, light_qkv[1:], preferred_element_type=jnp.float32
    ).astype(jnp.bfloat16)
    paired = padded(paired, (("seq", 1),), RADIUS)
    key_rows = paired[0]
    value_rows = paired[1]
    block_rows = min(512, local_rows)
    first_row = shard_index * local_rows
    query_pos = first_row + 0 + jnp.arange(block_rows, dtype=jnp.int32)
    key_pos = first_row + 0 - RADIUS + jnp.arange(block_rows + 2 * RADIUS, dtype=jnp.int32)
    distance = jnp.abs(query_pos[:, None] - key_pos[None, :])
    allowed = (
        (distance <= RADIUS)
        & (key_pos[None, :] >= 0)
        & (key_pos[None, :] < local_rows * shard_total)
    )
    outputs = mix_heads(queries, key_rows, value_rows, allowed)
    light_part = jnp.dot(outputs, light_out, preferred_element_type=jnp.float32)
    slot_range = jnp.arange(capacity, dtype=jnp.int32)
    query_live = slot_range < query_count[0]
    key_live = (slot_range < key_count[0]).astype(jnp.bfloat16)
    query_inputs = features[query_slots[0]]
    key_inputs = features[key_slots[0]]
    portion = lax.all_gather(heavy_qkv, "seq", axis=1, tiled=True)
    heavy_query = jnp.dot(query_inputs, portion[0], preferred_element_type=jnp.float32)
    heavy_key = jnp.dot(key_inputs, portion[1], preferred_element_type=jnp.float32)
    heavy_value = jnp.dot(key_inputs, portion[2], preferred_element_type=jnp.float32)
    heavy_query = heavy_query.astype(jnp.bfloat16)
    heavy_key = heavy_key.astype(jnp.bfloat16)
    heavy_value = heavy_value.astype(jnp.bfloat16)
    head_count = heavy_query.shape[1] // HEAD_DIM
    scale = HEAD_DIM ** (-0.5)
    query_heads = heavy_query.reshape(capacity, head_count, HEAD_DIM)
    row_peak = jnp.full((capacity, head_count), NEG, jnp.float32)
    key_part = lax.all_gather(heavy_key, "seq", axis=0, tiled=True)
    value_part = lax.all_gather(heavy_value, "seq", axis=0, tiled=True)
    live_part = lax.all_gather(key_live, "seq", axis=0, tiled=True)
    length = key_part.shape[0]
    key_heads = key_part.reshape(length, head_count, HEAD_DIM)
    value_heads = value_part.reshape(length, head_count, HEAD_DIM)
    live = live_part[None, None, :] > 0
    scores = (
        jnp.einsum("qhe,khe->qhk", query_heads, key_heads, preferred_element_type=jnp.float32)
        * scale
    )
    scores = jnp.where(live, scores, NEG)
    new_peak = jnp.maximum(row_peak, jnp.max(scores, axis=2))
    weights = jnp.where(live, jnp.exp(scores - new_peak[:, :, None]), 0.0)
    row_total = jnp.sum(weights, axis=2)
    blended = jnp.einsum(
        "qhk,khe->qhe",
        weights.astype(jnp.bfloat16),
        value_heads,
        preferred_element_type=jnp.float32,
    )
    row_peak, row_total, blended = (new_peak, row_total, blended)
    blended = blended / row_total[:, :, None]
    heavy_context = blended.reshape(capacity, head_count * HEAD_DIM).astype(jnp.bfloat16)
    gate = jax.nn.sigmoid(jnp.dot(query_inputs, router, preferred_element_type=jnp.float32))
    gate = jnp.where(query_live, gate, 0.0)
    heavy_rows = (
        jnp.dot(
            heavy_context,
            lax.all_gather(heavy_out, "seq", axis=1, tiled=True),
            preferred_element_type=jnp.float32,
        )
        * gate[:, None]
    )
    combined = light_part.at[query_slots[0]].add(heavy_rows)
    return lax.psum_scatter(combined, "mp", scatter_dimension=1, tiled=True).astype(jnp.bfloat16)


def solution(mesh):
    in_specs = (
        P("seq", "mp"),
        P(),
        P(None, None, "mp"),
        P("mp", None),
        P(None, "seq", "mp"),
        P("mp", "seq"),
        P("seq", None),
        P("seq"),
        P("seq", None),
        P("seq"),
    )
    out_specs = P("seq", "mp")
    return jax.shard_map(shards, mesh=mesh, in_specs=in_specs, out_specs=out_specs, check_vma=False)
```

profile of v0, /device:TPU:1, one launch (start us, length us, event | category | flops | bytes accessed | tf_op | source)
XLA Modules:
  0.0 995.2 jit_solution(5200214284138071772)
XLA Ops:
  6.5 0.0 copy-start
  6.5 0.0 copy-start.7
  6.5 0.0 all-gather.6.cloned.1.call-start
  6.6 0.7 all-gather.6.cloned.1.call-update
  7.3 0.0 all-gather.8.cloned.1.call-start
  7.3 0.7 all-gather.8.cloned.1.call-update
  8.0 0.0 all-gather.12.cloned.1.call-start
  8.1 0.7 fusion.72
  8.7 43.7 %all-gather.6.cloned.1.call-done = bf16[512,2048]{1,0:T(8,128)(2,1)} async-done(((bf16[512,1024]{1,0:T(8,128)(2,1)}), bf16[512,2048]{1,0:T(8,128)(2,1)}) %all-gather.6.cloned.1.call-update) | async-done | bytes 2097168 | tf_op jit(solution)/shard_map/all_gather | solution.py:67
  52.5 2.6 gather_fusion
  55.1 215.8 %all-gather.8.cloned.1.call-done = bf16[3,2048,512]{2,1,0:T(8,128)(2,1)} async-done(((bf16[3,16,512]{2,1,0:T(8,128)(2,1)}), bf16[3,2048,512]{2,1,0:T(8,128)(2,1)}) %all-gather.8.cloned.1.call-update) | async-done | bytes 6291472 | tf_op jit(solution)/shard_map/all_gather | solution.py:94
  270.9 2.7 fusion.56
  273.5 0.0 all-gather.12.cloned.1.call-update
  273.6 0.0 all-gather.10.cloned.1.call-start
  273.6 2.7 fusion.54
  276.3 0.0 all-gather.10.cloned.1.call-update
  276.3 0.0 all-gather.14.cloned.1.call-start
  276.4 0.5 all-gather.14.cloned.1.call-update
  276.9 0.0 reduce-scatter.2.cloned.1.call-start
  278.3 0.0 copy-done.6
  278.3 0.0 copy-start.4
  278.4 0.0 copy-done.3
  278.4 0.0 copy-done.7
  278.4 0.6 dynamic-slice
  279.6 0.2 dynamic-update-slice
  279.9 280.5 %all-reduce = bf16[4096]{0:T(1024)(128)(2,1)S(1)} all-reduce(bf16[4096]{0:T(1024)(128)(2,1)S(1)} %dynamic-update-slice), channel_id=1, replica_groups=mesh['seq'=128,'mp'=2] {'seq'}, use_global_device_ids=true, to_apply=%add | all-reduce | flops 4096 | bytes 16384
  560.4 0.0 copy-done.4
  560.4 1.2 fusion.42
  561.7 5.3 fusion.30
  567.0 0.7 fusion.77
  567.7 1.9 collective-permute-start
  569.6 3.9 collective-permute-start.1
  573.5 0.0 copy-done.2
  573.5 3.8 fusion.43
  577.3 2.6 gather_fusion.1
  579.9 0.1 fusion.61
  580.1 0.0 collective-permute-done
  580.1 0.0 collective-permute-done.1
  580.1 0.1 pad_maximum_fusion
  580.2 0.1 fusion.76
  580.3 1.1 copy.17
  581.4 0.3 copy.16
  581.7 8.4 fusion.78
  590.1 4.2 fusion.46
  594.3 0.0 copy-done
  594.3 3.3 fusion.80
  597.6 2.0 fusion.55
  599.7 0.1 reshape.159
  599.8 0.0 all-gather.12.cloned.1.call-done
  599.8 6.7 copy.19
  606.5 96.9 %all-gather.10.cloned.1.call-done = bf16[4096,512]{1,0:T(8,128)(2,1)} async-done(((bf16[32,512]{1,0:T(8,128)(2,1)}), bf16[4096,512]{1,0:T(8,128)(2,1)}) %all-gather.10.cloned.1.call-update) | async-done | bytes 4194320 | tf_op jit(solution)/shard_map/all_gather | solution.py:106
  703.4 6.5 copy.18
  709.9 3.2 fusion.79
  713.0 0.9 fusion.11
  713.9 1.3 copy-done.1
  715.2 1.3 fusion.65
  716.6 0.1 convert_element_type.54
  716.7 201.3 %all-gather.14.cloned.1.call-done = bf16[512,2048]{0,1:T(8,128)(2,1)} async-done(((bf16[512,16]{0,1:T(8,128)(2,1)}), bf16[512,2048]{0,1:T(8,128)(2,1)}) %all-gather.14.cloned.1.call-update) | async-done | bytes 2097168 | tf_op jit(solution)/shard_map/all_gather | solution.py:134
  918.0 2.3 convolution_multiply_fusion.1
  920.3 0.0 copy-done.5
  920.4 5.1 scatter_fusion
  925.5 0.0 reduce-scatter.2.cloned.1.call-update
  925.5 60.1 %reduce-scatter.2.cloned.1.call-done = f32[512,1024]{1,0:T(8,128)} async-done(((f32[512,2048]{1,0:T(8,128)}), f32[512,1024]{1,0:T(8,128)}) %reduce-scatter.2.cloned.1.call-update) | async-done | bytes 2097168 | tf_op jit(solution)/shard_map/reduce_scatter | solution.py:140
  985.6 2.7 convert_element_type.55
  (17 shorter events, 0.1 us)
Async XLA Ops:
  6.5 587.8 %copy-start = (bf16[512,2048]{1,0:T(8,128)(2,1)S(1)}, bf16[512,2048]{1,0:T(8,128)(2,1)}, u32[]{:S(2)}) copy-start(bf16[512,2048]{1,0:T(8,128)(2,1)} %param.13) | copy-start | bytes 6291460
  6.5 271.8 %copy-start.7 = (u32[256]{0:T(256)S(1)}, u32[256]{0:T(256)}, u32[]{:S(2)}) copy-start(u32[256]{0:T(256)} %constant.41) | copy-start | bytes 3076
  6.5 271.8 %copy-start.6 = (s32[1,32]{1,0:T(1,128)S(1)}, s32[1,32]{1,0:T(1,128)}, u32[]{:S(2)}) copy-start(s32[1,32]{1,0:T(1,128)} %param.16) | copy-start | bytes 388
  6.5 271.8 %copy-start.3 = (bf16[2048]{0:T(1024)(128)(2,1)S(1)}, bf16[2048]{0:T(1024)(128)(2,1)}, u32[]{:S(2)}) copy-start(bf16[2048]{0:T(1024)(128)(2,1)} %param.11) | copy-start | bytes 12292
  6.5 45.9 %all-gather.6.cloned.1.call-start = ((), (), s32[]{:S(2)}) async-start(), calls=%async_computation.1 | async-start | bytes 3145728 | tf_op jit(solution)/shard_map/all_gather | solution.py:67
  7.3 263.6 %all-gather.8.cloned.1.call-start = ((), (), s32[]{:S(2)}) async-start(), calls=%async_computation.2 | async-start | bytes 6340608 | tf_op jit(solution)/shard_map/all_gather | solution.py:94
  8.0 591.8 %all-gather.12.cloned.1.call-start = ((), (), s32[]{:S(2)}) async-start(), calls=%async_computation.4 | async-start | bytes 4227072 | tf_op jit(solution)/shard_map/all_gather | solution.py:105
  273.6 429.8 %all-gather.10.cloned.1.call-start = ((), (), s32[]{:S(2)}) async-start(), calls=%async_computation.3 | async-start | bytes 4227072 | tf_op jit(solution)/shard_map/all_gather | solution.py:106
  276.3 641.7 %all-gather.14.cloned.1.call-start = ((), (), s32[]{:S(2)}) async-start(), calls=%async_computation.5 | async-start | bytes 2113536 | tf_op jit(solution)/shard_map/all_gather | solution.py:134
  276.9 708.7 %reduce-scatter.2.cloned.1.call-start = ((), (), s32[]{:S(2)}) async-start(), calls=%async_computation.6 | async-start | bytes 6291456 | tf_op jit(solution)/shard_map/reduce_scatter | solution.py:140
  278.3 282.1 %copy-start.4 = (s32[32]{0:T(128)}, s32[32]{0:T(128)S(1)}, u32[]{:S(2)}) copy-start(s32[32]{0:T(128)S(1)} %fusion.71) | copy-start | bytes 388
  561.7 11.9 %copy-start.2 = (bf16[512,2048]{1,0:T(8,128)(2,1)S(1)}, bf16[512,2048]{1,0:T(8,128)(2,1)}, u32[]{:S(2)}) copy-start(bf16[512,2048]{1,0:T(8,128)(2,1)} %all-gather.6.cloned.1.call-done) | copy-start | bytes 6291460
  567.7 12.4 %collective-permute-start = (bf16[2,64,512]{2,1,0:T(8,128)(2,1)}, bf16[2,64,512]{2,1,0:T(8,128)(2,1)S(1)}, u32[]{:S(2)}, u32[]{:S(2)}) collective-permute-start(bf16[2,64,512]{2,1,0:T(8,128)(2,1)} %get-tuple-element.7), channel_id=1, source_target_pairs={{0,2},{2,4},{4,6},{6,8},{8,10},{10,12},{12,14},{14,16},{16,18},{18... | collective-permute-start | bytes 393224 | tf_op jit(solution)/shard_map/ppermute | solution.py:19
  569.6 10.5 %collective-permute-start.1 = (bf16[2,64,512]{2,1,0:T(8,128)(2,1)}, bf16[2,64,512]{2,1,0:T(8,128)(2,1)S(1)}, u32[]{:S(2)}, u32[]{:S(2)}) collective-permute-start(bf16[2,64,512]{2,1,0:T(8,128)(2,1)} %get-tuple-element.8), channel_id=1, source_target_pairs={{2,0},{4,2},{6,4},{8,6},{10,8},{12,10},{14,12},{16,14},{18,16},{20... | collective-permute-start | bytes 393224 | tf_op jit(solution)/shard_map/ppermute | solution.py:21
  713.0 2.2 copy-start.1
  715.2 205.1 %copy-start.5 = (s32[32]{0:T(128)S(1)}, s32[32]{0:T(128)}, u32[]{:S(2)}) copy-start(s32[32]{0:T(128)} %copy-done.4) | copy-start | bytes 388
Sparse Core Ops, SparseCore 0:
  9.1 43.2 all-gather.5
  54.4 216.4 all-gather.7
  273.7 213.8 all-gather.11
  489.3 214.0 all-gather.9
  705.1 212.8 all-gather.13
  925.6 59.9 reduce-scatter.1
where the time goes:
time: 996 us; the launch traced here: 995 us
  waiting for transfers between devices  620 us (62%)
  blocking collectives  281 us (28%)
  matrix products  39.3 us (4%)
  local copies, waits for them, and re-layouts  23 us (2%)
  between operations  15.7 us (2%)
  other arithmetic  10.8 us (1%)
    unnamed x1, blocking collectives  281 us
    all_gather x1, waiting for transfers between devices, shards(): portion = lax.all_gather(heavy_qkv, 'seq', axis=1, tiled=True)  216 us
    all_gather x1, waiting for transfers between devices, shards(): lax.all_gather(heavy_out, 'seq', axis=1, tiled=True)  201 us
    all_gather x1, waiting for transfers between devices, shards(): value_part = lax.all_gather(heavy_value, 'seq', axis=0, tiled=True)  96.9 us
    reduce_scatter x1, waiting for transfers between devices, shards(): lax.psum_scatter(combined, 'mp', scatter_dimension=1, tiled=True)  60.1 us
    all_gather x1, waiting for transfers between devices, shards(): features = lax.all_gather(normed, 'mp', axis=1, tiled=True)  43.7 us
  transfers between devices with their start and end apart: 8, of which 5 were waited for; matrix products, arithmetic and copies ran while one was open for 6% of the time, Pallas kernels for 0%

commit v1 on v0

--- a/solution.py
+++ b/solution.py
@@ -131,7 +131,9 @@
     heavy_rows = (
         jnp.dot(
             heavy_context,
-            lax.all_gather(heavy_out, "seq", axis=1, tiled=True),
+            jnp.concatenate(
+                lax.all_to_all(jnp.stack([heavy_out] * lax.axis_size("seq")), "seq", 0, 0), axis=1
+            ),
             preferred_element_type=jnp.float32,
         )
         * gate[:, None]

time: 996 us -> 800 us (0.80)
  waiting for transfers between devices: 620 us -> 374 us
  blocking collectives: 281 us -> 318 us
  starting transfers between devices: 6.05 us -> 16.1 us
    all_gather x1 -> x0, waiting for transfers between devices: 201 us -> none  [shards(): lax.all_gather(heavy_out, 'seq', axis=1, tiled=True)]
    all_gather x1, waiting for transfers between devices: 96.9 us -> 53.2 us  [shards(): value_part = lax.all_gather(heavy_value, 'seq', axis=0, tiled=True)]
    unnamed x1, blocking collectives: 281 us -> 318 us
    all_to_all x0 -> x1, starting transfers between devices: none -> 10.5 us  [shards(): lax.all_to_all(jnp.stack([heavy_out] * lax.axis_size('seq')), 'seq', 0, 0)]
  transfers between devices with their start and end apart: 8 -> 8, of which waited for: 5 -> 4; matrix products, arithmetic and copies ran while one was open for 6% -> 8% of each run, Pallas kernels for 0% -> 0%
where the time goes in v1:
time: 800 us; the launch traced here: 799 us
  waiting for transfers between devices  374 us (47%)
  blocking collectives  318 us (40%)
  matrix products  39.3 us (5%)
  local copies, waits for them, and re-layouts  25.2 us (3%)
  starting transfers between devices  16.1 us (2%)
  between operations  15.4 us (2%)
  other arithmetic  10.8 us (1%)
    unnamed x1, blocking collectives  318 us
    all_gather x1, waiting for transfers between devices, shards(): portion = lax.all_gather(heavy_qkv, 'seq', axis=1, tiled=True)  216 us
    reduce_scatter x1, waiting for transfers between devices, shards(): lax.psum_scatter(combined, 'mp', scatter_dimension=1, tiled=True)  60.2 us
    all_gather x1, waiting for transfers between devices, shards(): value_part = lax.all_gather(heavy_value, 'seq', axis=0, tiled=True)  53.2 us
    all_gather x1, waiting for transfers between devices, shards(): features = lax.all_gather(normed, 'mp', axis=1, tiled=True)  43.7 us
  transfers between devices with their start and end apart: 8, of which 4 were waited for; matrix products, arithmetic and copies ran while one was open for 8% of the time, Pallas kernels for 0%

profile of v1, /device:TPU:1, one launch (start us, length us, event | category | flops | bytes accessed | tf_op | source)
XLA Modules:
  0.0 798.9 jit_solution(1919865420346143979)
XLA Ops:
  6.5 0.0 copy-start
  6.5 0.0 all-gather.5.cloned.1.call-start
  6.5 0.7 all-gather.5.cloned.1.call-update
  7.3 0.0 all-gather.7.cloned.1.call-start
  7.3 0.7 all-gather.7.cloned.1.call-update
  8.0 0.0 all-gather.11.cloned.1.call-start
  8.1 0.7 fusion.72
  8.7 43.7 %all-gather.5.cloned.1.call-done = bf16[512,2048]{1,0:T(8,128)(2,1)} async-done(((bf16[512,1024]{1,0:T(8,128)(2,1)}), bf16[512,2048]{1,0:T(8,128)(2,1)}) %all-gather.5.cloned.1.call-update) | async-done | bytes 2097168 | tf_op jit(solution)/shard_map/all_gather | solution.py:67
  52.5 2.6 gather_fusion
  55.1 215.8 %all-gather.7.cloned.1.call-done = bf16[3,2048,512]{2,1,0:T(8,128)(2,1)} async-done(((bf16[3,16,512]{2,1,0:T(8,128)(2,1)}), bf16[3,2048,512]{2,1,0:T(8,128)(2,1)}) %all-gather.7.cloned.1.call-update) | async-done | bytes 6291472 | tf_op jit(solution)/shard_map/all_gather | solution.py:94
  270.9 2.7 fusion.56
  273.5 0.0 all-gather.11.cloned.1.call-update
  273.6 0.0 copy-start.4
  273.6 0.0 copy-start.8
  273.6 0.0 copy-start.7
  273.6 0.0 all-gather.9.cloned.1.call-start
  273.7 2.7 fusion.54
  276.3 0.0 all-gather.9.cloned.1.call-update
  276.4 0.0 copy-done.3
  276.4 1.6 stack.2
  278.0 10.5 %all-to-all-start = ((bf16[128,512,16]{1,2,0:T(8,128)(2,1)}), bf16[128,512,16]{1,2,0:T(8,128)(2,1)}, u32[]{:S(2)}, u32[]{:S(2)}) async-start(bf16[128,512,16]{1,2,0:T(8,128)(2,1)} %stack.2), calls=%async_computation | async-start | bytes 4194304 | tf_op jit(solution)/shard_map/all_to_all | solution.py:135
  288.5 0.0 reduce-scatter.2.cloned.1.call-start
  289.9 0.0 copy-done.4
  289.9 0.0 copy-done.8
  289.9 0.7 dynamic-slice
  291.3 0.2 dynamic-update-slice
  291.5 317.7 %all-reduce = bf16[4096]{0:T(1024)(128)(2,1)S(1)} all-reduce(bf16[4096]{0:T(1024)(128)(2,1)S(1)} %dynamic-update-slice), channel_id=1, replica_groups=mesh['seq'=128,'mp'=2] {'seq'}, use_global_device_ids=true, to_apply=%add | all-reduce | flops 4096 | bytes 16384
  609.3 0.0 copy-done.7
  609.3 0.4 copy-done.5
  609.8 1.3 fusion.42
  611.0 5.3 fusion.30
  616.3 0.7 fusion.77
  617.0 1.9 collective-permute-start
  619.0 3.6 collective-permute-start.1
  622.5 3.7 fusion.43
  626.2 2.6 gather_fusion.1
  628.9 0.1 fusion.61
  629.0 0.0 collective-permute-done
  629.0 0.0 collective-permute-done.1
  629.1 0.1 pad_maximum_fusion
  629.2 0.1 fusion.76
  629.2 1.1 copy.18
  630.3 0.3 copy.17
  630.6 8.4 %fusion.78 = (f32[8,512]{1,0:T(8,128)S(1)}, bf16[8,512,640]{2,1,0:T(8,128)(2,1)}) fusion(pred[512,640]{1,0:T(8,128)(4,1)} %fusion.42, bf16[512,8,64]{0,2,1:T(8,128)(2,1)} %bitcast.101, bf16[640,8,64]{0,2,1:T(8,128)(2,1)} %bitcast.98), kind=kOutput, calls=%fused_computation.77 | convolution fusion | flops 351273600 | bytes 6766592 | tf_op jit(solution)/shard_map/sub | solution.py:39
  639.1 4.2 fusion.46
  643.3 3.3 fusion.80
  646.6 2.0 fusion.55
  648.6 0.1 reshape.167
  648.8 0.0 all-gather.11.cloned.1.call-done
  648.8 6.7 copy.20
  655.4 53.2 %all-gather.9.cloned.1.call-done = bf16[4096,512]{1,0:T(8,128)(2,1)} async-done(((bf16[32,512]{1,0:T(8,128)(2,1)}), bf16[4096,512]{1,0:T(8,128)(2,1)}) %all-gather.9.cloned.1.call-update) | async-done | bytes 4194320 | tf_op jit(solution)/shard_map/all_gather | solution.py:106
  708.6 6.5 copy.19
  715.1 3.2 fusion.79
  718.3 0.9 fusion.11
  719.2 1.3 copy-done.1
  720.5 1.3 fusion.65
  721.8 0.1 convert_element_type.54
  721.9 0.0 all-to-all-done
  722.0 2.3 convolution_multiply_fusion.1
  724.2 0.0 copy-done.6
  724.3 5.1 scatter_fusion
  729.4 0.0 reduce-scatter.2.cloned.1.call-update
  729.4 60.2 %reduce-scatter.2.cloned.1.call-done = f32[512,1024]{1,0:T(8,128)} async-done(((f32[512,2048]{1,0:T(8,128)}), f32[512,1024]{1,0:T(8,128)}) %reduce-scatter.2.cloned.1.call-update) | async-done | bytes 2097168 | tf_op jit(solution)/shard_map/reduce_scatter | solution.py:142
  789.7 2.7 convert_element_type.55
  (19 shorter events, 0.1 us)
Async XLA Ops:
  6.5 636.8 %copy-start = (bf16[512,2048]{1,0:T(8,128)(2,1)S(1)}, bf16[512,2048]{1,0:T(8,128)(2,1)}, u32[]{:S(2)}) copy-start(bf16[512,2048]{1,0:T(8,128)(2,1)} %param.13) | copy-start | bytes 6291460
  6.5 269.8 %copy-start.3 = (bf16[512,16]{0,1:T(8,128)(2,1)S(1)}, bf16[512,16]{0,1:T(8,128)(2,1)}, u32[]{:S(2)}) copy-start(bf16[512,16]{0,1:T(8,128)(2,1)} %param.15) | copy-start | bytes 49156
  6.5 45.9 %all-gather.5.cloned.1.call-start = ((), (), s32[]{:S(2)}) async-start(), calls=%async_computation.2 | async-start | bytes 3145728 | tf_op jit(solution)/shard_map/all_gather | solution.py:67
  7.3 263.6 %all-gather.7.cloned.1.call-start = ((), (), s32[]{:S(2)}) async-start(), calls=%async_computation.3 | async-start | bytes 6340608 | tf_op jit(solution)/shard_map/all_gather | solution.py:94
  8.0 640.8 %all-gather.11.cloned.1.call-start = ((), (), s32[]{:S(2)}) async-start(), calls=%async_computation.5 | async-start | bytes 4227072 | tf_op jit(solution)/shard_map/all_gather | solution.py:105
  273.6 16.3 %copy-start.4 = (bf16[2048]{0:T(1024)(128)(2,1)S(1)}, bf16[2048]{0:T(1024)(128)(2,1)}, u32[]{:S(2)}) copy-start(bf16[2048]{0:T(1024)(128)(2,1)} %param.11) | copy-start | bytes 12292
  273.6 16.3 %copy-start.8 = (u32[256]{0:T(256)S(1)}, u32[256]{0:T(256)}, u32[]{:S(2)}) copy-start(u32[256]{0:T(256)} %constant.41) | copy-start | bytes 3076
  273.6 335.7 %copy-start.7 = (s32[1,32]{1,0:T(1,128)S(1)}, s32[1,32]{1,0:T(1,128)}, u32[]{:S(2)}) copy-start(s32[1,32]{1,0:T(1,128)} %param.16) | copy-start | bytes 388
  273.6 435.0 %all-gather.9.cloned.1.call-start = ((), (), s32[]{:S(2)}) async-start(), calls=%async_computation.4 | async-start | bytes 4227072 | tf_op jit(solution)/shard_map/all_gather | solution.py:106
  278.0 444.0 %all-to-all-start = ((bf16[128,512,16]{1,2,0:T(8,128)(2,1)}), bf16[128,512,16]{1,2,0:T(8,128)(2,1)}, u32[]{:S(2)}, u32[]{:S(2)}) async-start(bf16[128,512,16]{1,2,0:T(8,128)(2,1)} %stack.2), calls=%async_computation | async-start | bytes 4194304 | tf_op jit(solution)/shard_map/all_to_all | solution.py:135
  288.5 501.2 %reduce-scatter.2.cloned.1.call-start = ((), (), s32[]{:S(2)}) async-start(), calls=%async_computation.6 | async-start | bytes 6291456 | tf_op jit(solution)/shard_map/reduce_scatter | solution.py:142
  609.3 0.5 copy-start.5
  611.0 11.5 %copy-start.2 = (bf16[512,2048]{1,0:T(8,128)(2,1)S(1)}, bf16[512,2048]{1,0:T(8,128)(2,1)}, u32[]{:S(2)}) copy-start(bf16[512,2048]{1,0:T(8,128)(2,1)} %all-gather.5.cloned.1.call-done) | copy-start | bytes 6291460
  617.0 12.0 %collective-permute-start = (bf16[2,64,512]{2,1,0:T(8,128)(2,1)}, bf16[2,64,512]{2,1,0:T(8,128)(2,1)S(1)}, u32[]{:S(2)}, u32[]{:S(2)}) collective-permute-start(bf16[2,64,512]{2,1,0:T(8,128)(2,1)} %get-tuple-element.7), channel_id=1, source_target_pairs={{0,2},{2,4},{4,6},{6,8},{8,10},{10,12},{12,14},{14,16},{16,18},{18... | collective-permute-start | bytes 393224 | tf_op jit(solution)/shard_map/ppermute | solution.py:19
  619.0 10.1 %collective-permute-start.1 = (bf16[2,64,512]{2,1,0:T(8,128)(2,1)}, bf16[2,64,512]{2,1,0:T(8,128)(2,1)S(1)}, u32[]{:S(2)}, u32[]{:S(2)}) collective-permute-start(bf16[2,64,512]{2,1,0:T(8,128)(2,1)} %get-tuple-element.8), channel_id=1, source_target_pairs={{2,0},{4,2},{6,4},{8,6},{10,8},{12,10},{14,12},{16,14},{18,16},{20... | collective-permute-start | bytes 393224 | tf_op jit(solution)/shard_map/ppermute | solution.py:21
  718.3 2.2 copy-start.1
  720.5 3.8 copy-start.6
Sparse Core Ops, SparseCore 0:
  9.1 43.2 all-gather.4
  54.3 216.4 all-gather.6
  273.7 218.5 all-gather.10
  494.0 214.5 all-gather.8
  729.6 60.0 reduce-scatter.1
